TPU v7x, 32 devices: a whole 2x2x4 slice. The times are simulated.
32 devices in a mesh: groups: 2 (over y), rows: 4 (over z), cols: 4 (over x, core).
Axes of the slice: x: 2, y: 2, z: 4, core: 2. Of those that a mesh axis runs over, the one named last changes fastest.
Arguments:
- tokens: bfloat16 [128, 256, 512], P(('groups', 'rows'), 'cols'), parts along dimension 0, may hold values from -30 to 30
- qkv_weight: bfloat16 [512, 1536], replicated, may hold values from -0.25 to 0.25
- depth_kernel: float32 [25, 1536], replicated, may hold values from -1.25 to 1.25
- group_kernel: bfloat16 [48, 32, 32], replicated, may hold values from -1 to 1
- proj_weight: bfloat16 [1024, 512], replicated, may hold values from -0.1875 to 0.1875
- out_gain: float32 [512], replicated, may hold values from 4 to 16
- out_bias: float32 [512], replicated, may hold values from -3 to 3
Outputs:
- output: bfloat16 [128, 256, 512], P(('groups', 'rows'), 'cols'), parts along dimension 0
There are 2 independent parts, one for each index of `groups`. A program takes and returns all parts, laid end to end along the dimension named above; an argument that names none is the same for every part. Nothing has to cross between parts.
All inputs are finite; a program needn't handle non-finite values.
Results may differ from a plain program's by a relative error of at most 0.0048.
Values may be sent and summed in bfloat16 or wider, within the bound.
A program may use at most 64 MiB of HBM per device.

v0:
```python
import jax
import jax.numpy as jnp
from jax import lax
from jax.sharding import PartitionSpec as P

HEAD_DIM = 32


def padded_2(value, sides, width):
    for axis, dim in sides:
        size, length = (lax.axis_size(axis), value.shape[dim])
        up = [(i, (i + 1) % size) for i in range(size - 1)]
        down = [(j, i) for i, j in up]
        last = lax.slice_in_dim(value, length - width, length, axis=dim)
        leading = lax.slice_in_dim(value, 0, width, axis=dim)
        before = lax.ppermute(last, axis, up)
        after = lax.ppermute(leading, axis, down)
        value = jnp.concatenate([before, value, after], axis=dim)
    return value


def feature_map(inputs):
    return jax.nn.elu(inputs.astype(jnp.float32)) + 1.0


def aggregate(padded, depth_kernel, group_kernel, height, breadth):
    channels = padded.shape[2]
    summed = jnp.zeros((height, breadth, channels), jnp.float32)
    for offset_row in range(5):
        for offset_col in range(5):
            window = padded[offset_row : offset_row + height, offset_col : offset_col + breadth]
            summed = summed + window * depth_kernel[offset_row * 5 + offset_col]
    spread = summed.astype(jnp.bfloat16).reshape(height * breadth, channels // HEAD_DIM, HEAD_DIM)
    grouped = jnp.einsum("ngc,gcd->ngd", spread, group_kernel, preferred_element_type=jnp.float32)
    return grouped.astype(jnp.bfloat16).reshape(height * breadth, channels)


def context_states(source):
    amount = source.shape[0]
    grouped = source.reshape(amount, -1, 3, HEAD_DIM)
    key_feats = feature_map(grouped[:, :, 1]).astype(jnp.bfloat16)
    values = grouped[:, :, 2]
    states = jnp.einsum("nhd,nhe->hde", key_feats, values, preferred_element_type=jnp.float32)
    totals = jnp.sum(key_feats.astype(jnp.float32), axis=0)
    return (states, totals)


def body(tokens, qkv_weight, depth_kernel, group_kernel, proj_weight, out_gain, out_bias):
    height, breadth, channels = tokens.shape
    amount = height * breadth
    triple = jnp.dot(
        tokens.reshape(amount, channels), qkv_weight, preferred_element_type=jnp.float32
    )
    triple = triple.astype(jnp.bfloat16).reshape(height, breadth, 3 * channels)
    padded = padded_2(triple, (("rows", 0), ("cols", 1)), 2)
    flat_triple = triple.reshape(amount, 3 * channels)
    plain_state, plain_total = context_states(flat_triple)
    aggregated = aggregate(padded, depth_kernel, group_kernel, height, breadth)
    scaled_state, scaled_total = context_states(aggregated)
    states, totals = lax.psum(
        (
            jnp.concatenate([plain_state, scaled_state], 0),
            jnp.concatenate([plain_total, scaled_total], 0),
        ),
        ("rows", "cols"),
    )
    queries = jnp.concatenate(
        [
            feature_map(flat_triple.reshape(amount, -1, 3, HEAD_DIM)[:, :, 0]),
            feature_map(aggregated.reshape(amount, -1, 3, HEAD_DIM)[:, :, 0]),
        ],
        1,
    )
    numerator = jnp.einsum("nhd,hde->nhe", queries, states, precision=lax.Precision.HIGHEST)
    denominator = jnp.einsum("nhd,hd->nh", queries, totals, precision=lax.Precision.HIGHEST)
    attended = (
        (numerator / denominator[:, :, None]).astype(jnp.bfloat16).reshape(amount, 2 * channels)
    )
    projected = jnp.dot(attended, proj_weight, preferred_element_type=jnp.float32)
    result = tokens.reshape(amount, channels).astype(jnp.float32) + out_gain * projected + out_bias
    return result.astype(jnp.bfloat16).reshape(height, breadth, channels)


def solution(mesh):
    placed = (P(("groups", "rows"), "cols", None), P(), P(), P(), P(), P(), P())
    return jax.shard_map(
        body,
        mesh=mesh,
        in_specs=placed,
        out_specs=P(("groups", "rows"), "cols", None),
        check_vma=False,
    )
```

profile of v0, /device:TPU:0, one launch (start us, length us, event | category | flops | bytes accessed | tf_op | source)
XLA Modules:
  0.0 203.0 jit_solution(8702821918944475526)
XLA Ops:
  6.5 1.4 copy-done
  7.9 3.0 %convolution_convert_fusion = bf16[1024,1536]{1,0:T(8,128)(2,1)S(1)} fusion(bf16[1024,512]{1,0:T(8,128)(2,1)} %bitcast.85, bf16[512,1536]{1,0:T(8,128)(2,1)S(1)} %copy-done), kind=kOutput, calls=%fused_computation.14 | convolution fusion | flops 1612185600 | bytes 5767168 | tf_op jit(solution)/shard_map/dot_general | solution.py:51
  11.0 1.7 copy-done.1
  12.6 0.1 fusion.25
  12.7 4.9 %collective-permute-start = (bf16[2,64,1536]{2,1,0:T(8,128)(2,1)S(1)}, bf16[2,64,1536]{2,1,0:T(8,128)(2,1)S(1)}, u32[]{:S(2)}, u32[]{:S(2)}) collective-permute-start(bf16[2,64,1536]{2,1,0:T(8,128)(2,1)S(1)} %bitcast.82), channel_id=1, source_target_pairs={{0,4},{4,8},{8,12},{1,5},{5,9},{9,13},{2,6},{6,10},{10,14},{3,7},{... | collective-permute-start | bytes 1179656 | tf_op jit(solution)/shard_map/ppermute | solution.py:16
  17.6 1.3 collective-permute-start.1
  18.9 4.7 %copy.26 = bf16[1024,1536]{0,1:T(8,128)(2,1)} copy(bf16[1024,1536]{1,0:T(8,128)(2,1)} %copy-done.1) | data formatting | bytes 6291456 | tf_op jit(solution)/shard_map/convert_element_type | solution.py:54
  23.7 3.5 %fusion.16 = f32[16,32,32]{2,1,0:T(8,128)} fusion(bf16[1024,16,3,32]{0,3,2,1:T(8,128)(2,1)} %bitcast.77), kind=kOutput, calls=%fused_computation.45 | convolution fusion | flops 36700160 | bytes 2162688 | tf_op jit(solution)/shard_map/nhd,nhe->hde/dot_general | solution.py:43
  27.2 3.0 %collective-permute-done.1 = bf16[2,64,1536]{2,1,0:T(8,128)(2,1)S(1)} collective-permute-done((bf16[2,64,1536]{2,1,0:T(8,128)(2,1)S(1)}, bf16[2,64,1536]{2,1,0:T(8,128)(2,1)S(1)}, u32[]{:S(2)}, u32[]{:S(2)}) %collective-permute-start.1) | collective-permute-done | bytes 393248 | tf_op jit(solution)/shard_map/ppermute | solution.py:17
  30.1 0.2 pad_maximum_fusion.11
  30.3 1.3 collective-permute-start.2
  31.6 1.5 collective-permute-start.3
  33.1 0.9 slice_reduce_fusion.24
  34.0 0.7 copy.29
  34.7 1.1 slice_reduce_fusion.23
  35.9 0.0 collective-permute-done.2
  35.9 0.6 collective-permute-done.3
  36.6 5.4 %maximum_maximum_fusion = (bf16[20,66,1536]{2,1,0:T(8,128)(2,1)S(1)}, bf16[20,66,1536]{2,1,0:T(8,128)(2,1)S(1)}) fusion(bf16[2,64,1536]{2,1,0:T(8,128)(2,1)S(1)} %collective-permute-done.1, bf16[16,64,1536]{2,1,0:T(8,128)(2,1)} %bitcast.74, bf16[2,64,1536]{2,1,0:T(8,128)(2,1)S(1)} %collective-permute-done, ...), kind=kLoop, calls=%fused_computation.9 | loop fusion | flops 32440320 | bytes 12288000 | tf_op jit(solution)/shard_map/concatenate | solution.py:18
  42.2 24.0 %add_convert_fusion = bf16[16,64,1536]{2,1,0:T(8,128)(2,1)} fusion(bf16[16,64,1536]{2,1,0:T(8,128)(2,1)S(1)} %bitcast.76, bf16[2,64,1536]{2,1,0:T(8,128)(2,1)S(1)} %collective-permute-done.1, bf16[2,64,1536]{2,1,0:T(8,128)(2,1)S(1)} %collective-permute-done, bf16[20,66,1536]{2,1,0:T(8,128)(2,1)S(1)} %get-tuple-element.31, ...), kind=kLoop, calls=%fused_computation.8 | loop fusion | flops 124256256 | bytes 70146048 | tf_op jit(solution)/shard_map/convert_element_type | solution.py:33
  66.2 8.6 %copy.28 = bf16[16,64,1536]{1,0,2:T(8,128)(2,1)} copy(bf16[16,64,1536]{2,1,0:T(8,128)(2,1)} %add_convert_fusion) | data formatting | bytes 6291456 | tf_op jit(solution)/shard_map/convert_element_type | solution.py:33
  74.8 9.4 %reshape.56 = bf16[1024,48,32]{0,2,1:T(8,128)(2,1)} reshape(bf16[16,64,1536]{1,0,2:T(8,128)(2,1)} %copy.28) | data formatting | bytes 6291456 | tf_op jit(solution)/shard_map/reshape | solution.py:33
  84.2 2.8 %convolution_convert_fusion.1 = bf16[48,1024,32]{1,2,0:T(8,128)(2,1)S(1)} fusion(bf16[48,32,32]{1,2,0:T(8,128)(2,1)S(1)} %copy.29, bf16[1024,48,32]{0,2,1:T(8,128)(2,1)} %reshape.56), kind=kOutput, calls=%fused_computation.25 | convolution fusion | flops 102236160 | bytes 6389760 | tf_op jit(solution)/shard_map/ngc,gcd->ngd/dot_general | solution.py:34
  87.0 1.1 fusion.15
  88.1 0.8 copy-done.4
  88.9 5.6 %fusion.12 = (f32[1024,16,32]{0,2,1:T(8,128)}, f32[16,32]{1,0:T(8,128)S(1)}, f32[16,32]{1,0:T(8,128)S(1)}, f32[1024,16,32]{0,2,1:T(8,128)}) fusion(bf16[1024,16,3,32]{0,3,2,1:T(8,128)(2,1)S(1)} %bitcast.78, bf16[1024,16,3,32]{0,3,2,1:T(8,128)(2,1)S(1)} %bitcast.80), kind=kLoop, calls=%fused_computation.33 | loop fusion | flops 13630464 | bytes 8392704 | tf_op jit(solution)/shard_map/add | solution.py:23
  94.5 0.8 pad_maximum_fusion.8
  95.3 0.0 all-reduce.2.cloned.1.call-update
  95.3 60.9 %psum.15 = f32[32,32]{1,0:T(8,128)S(1)} all-reduce(f32[32,32]{1,0:T(8,128)S(1)} %pad_maximum_fusion.12), channel_id=1, replica_groups=mesh['groups'=2,'rows'=4,'cols'=4] {'rows','cols'}, use_global_device_ids=true, to_apply=%region_3.4 | all-reduce | flops 1024 | bytes 8192 | tf_op jit(solution)/shard_map/psum | solution.py:60
  156.2 4.3 %fusion.1 = f32[32,1,1024]{2,1,0:T(1,128)S(1)} fusion(f32[32,32,1]{1,2,0:T(1,128)S(1)} %bitcast.84, f32[1024,16,32]{0,2,1:T(8,128)} %get-tuple-element.41, f32[1024,16,32]{0,2,1:T(8,128)} %get-tuple-element.34), kind=kOutput, calls=%fused_computation.19 | convolution fusion | flops 13631488 | bytes 4329472 | tf_op jit(solution)/shard_map/nhd,hd->nh/dot_general | solution.py:75
  160.6 27.5 %all-reduce.2.cloned.1.call-done = f32[32,32,32]{2,1,0:T(8,128)} async-done(((f32[32,32,32]{2,1,0:T(8,128)}), f32[32,32,32]{2,1,0:T(8,128)}) %all-reduce.2.cloned.1.call-update) | async-done | bytes 131088 | tf_op jit(solution)/shard_map/psum | solution.py:60
  188.1 5.8 %fusion = bf16[1024,32,32]{0,2,1:T(8,128)(2,1)S(1)} fusion(f32[1024,32]{0,1:T(8,128)S(1)} %bitcast.83, f32[32,32,32]{2,1,0:T(8,128)} %all-reduce.2.cloned.1.call-done, f32[1024,16,32]{0,2,1:T(8,128)} %get-tuple-element.41, f32[1024,16,32]{0,2,1:T(8,128)} %get-tuple-element.34), kind=kOutput, calls=%fused_computation.13 | convolution fusion | flops 405798912 | bytes 6553600 | tf_op jit(solution)/shard_map/nhd,hde->nhe/dot_general | solution.py:74
  193.9 2.3 %add_convert_fusion.1 = bf16[1024,512]{1,0:T(8,128)(2,1)} fusion(bf16[1024,512]{1,0:T(8,128)(2,1)S(1)} %bitcast.86, bf16[1024,1024]{0,1:T(8,128)(2,1)S(1)} %bitcast.87, bf16[1024,512]{1,0:T(8,128)(2,1)S(1)} %copy-done.22, f32[512]{0:T(512)S(1)} %copy-done.23, f32[512]{0:T(512)S(1)} %copy-done.24), kind=kOutput, calls=%fused_computation.36 | convolution fusion | flops 1076363264 | bytes 5246976 | tf_op jit(solution)/shard_map/dot_general | solution.py:79
  (51 shorter events, 0.1 us)
Async XLA Ops:
  6.5 1.4 copy-start
  6.5 181.5 %all-reduce.2.cloned.1.call-start = ((), (), s32[]{:S(2)}) async-start(), calls=%async_computation | async-start | bytes 1048576 | tf_op jit(solution)/shard_map/psum | solution.py:60
  11.0 1.7 copy-start.1
  12.7 14.5 %collective-permute-start = (bf16[2,64,1536]{2,1,0:T(8,128)(2,1)S(1)}, bf16[2,64,1536]{2,1,0:T(8,128)(2,1)S(1)}, u32[]{:S(2)}, u32[]{:S(2)}) collective-permute-start(bf16[2,64,1536]{2,1,0:T(8,128)(2,1)S(1)} %bitcast.82), channel_id=1, source_target_pairs={{0,4},{4,8},{8,12},{1,5},{5,9},{9,13},{2,6},{6,10},{10,14},{3,7},{... | collective-permute-start | bytes 1179656 | tf_op jit(solution)/shard_map/ppermute | solution.py:16
  17.6 12.5 %collective-permute-start.1 = (bf16[2,64,1536]{2,1,0:T(8,128)(2,1)S(1)}, bf16[2,64,1536]{2,1,0:T(8,128)(2,1)S(1)}, u32[]{:S(2)}, u32[]{:S(2)}) collective-permute-start(bf16[2,64,1536]{2,1,0:T(8,128)(2,1)S(1)} %bitcast.81), channel_id=1, source_target_pairs={{4,0},{8,4},{12,8},{5,1},{9,5},{13,9},{6,2},{10,6},{14,10},{7,3},{... | collective-permute-start | bytes 1179656 | tf_op jit(solution)/shard_map/ppermute | solution.py:17
  23.7 6.4 %copy-start.2 = (bf16[1024,1536]{1,0:T(8,128)(2,1)S(1)}, bf16[1024,1536]{1,0:T(8,128)(2,1)}, u32[]{:S(2)}) copy-start(bf16[1024,1536]{1,0:T(8,128)(2,1)} %copy-done.1) | copy-start | bytes 9437188
  23.7 9.4 %copy-start.7 = (f32[25,1536]{1,0:T(8,128)S(1)}, f32[25,1536]{1,0:T(8,128)}, u32[]{:S(2)}) copy-start(f32[25,1536]{1,0:T(8,128)} %param.9) | copy-start | bytes 460804
  23.7 10.3 %copy-start.5 = (bf16[48,32,32]{0,2,1:T(8,128)(2,1)S(1)}, bf16[48,32,32]{0,2,1:T(8,128)(2,1)}, u32[]{:S(2)}) copy-start(bf16[48,32,32]{0,2,1:T(8,128)(2,1)} %param.10) | copy-start | bytes 294916
  30.3 5.6 %collective-permute-start.2 = (bf16[20,2,1536]{2,1,0:T(2,128)(2,1)S(1)}, bf16[20,2,1536]{2,1,0:T(2,128)(2,1)S(1)}, u32[]{:S(2)}, u32[]{:S(2)}) collective-permute-start(bf16[20,2,1536]{2,1,0:T(2,128)(2,1)S(1)} %get-tuple-element.32), channel_id=1, source_target_pairs={{0,1},{1,2},{2,3},{4,5},{5,6},{6,7},{8,9},{9,10},{10,11},{12,13},{... | collective-permute-start | bytes 368648 | tf_op jit(solution)/shard_map/ppermute | solution.py:16
  31.6 4.9 %collective-permute-start.3 = (bf16[20,2,1536]{2,1,0:T(2,128)(2,1)S(1)}, bf16[20,2,1536]{2,1,0:T(2,128)(2,1)S(1)}, u32[]{:S(2)}, u32[]{:S(2)}) collective-permute-start(bf16[20,2,1536]{2,1,0:T(2,128)(2,1)S(1)} %get-tuple-element.33), channel_id=1, source_target_pairs={{1,0},{2,1},{3,2},{5,4},{6,5},{7,6},{9,8},{10,9},{11,10},{13,12},{... | collective-permute-start | bytes 368648 | tf_op jit(solution)/shard_map/ppermute | solution.py:17
  35.8 6.2 %copy-start.3 = (bf16[1024,1536]{1,0:T(8,128)(2,1)S(1)}, bf16[1024,1536]{1,0:T(8,128)(2,1)}, u32[]{:S(2)}) copy-start(bf16[1024,1536]{1,0:T(8,128)(2,1)} %copy-done.1) | copy-start | bytes 9437188
  35.8 6.2 %copy-start.8 = (f32[1536]{0:T(1024)S(1)}, f32[1536]{0:T(1024)}, u32[]{:S(2)}) copy-start(f32[1536]{0:T(1024)} %get-tuple-element.11) | copy-start | bytes 18436
  35.8 6.2 %copy-start.9 = (f32[1536]{0:T(1024)S(1)}, f32[1536]{0:T(1024)}, u32[]{:S(2)}) copy-start(f32[1536]{0:T(1024)} %get-tuple-element.12) | copy-start | bytes 18436
  35.8 6.2 %copy-start.10 = (f32[1536]{0:T(1024)S(1)}, f32[1536]{0:T(1024)}, u32[]{:S(2)}) copy-start(f32[1536]{0:T(1024)} %get-tuple-element.13) | copy-start | bytes 18436
  35.8 6.2 %copy-start.11 = (f32[1536]{0:T(1024)S(1)}, f32[1536]{0:T(1024)}, u32[]{:S(2)}) copy-start(f32[1536]{0:T(1024)} %get-tuple-element.14) | copy-start | bytes 18436
  35.8 6.2 %copy-start.12 = (f32[1536]{0:T(1024)S(1)}, f32[1536]{0:T(1024)}, u32[]{:S(2)}) copy-start(f32[1536]{0:T(1024)} %get-tuple-element.15) | copy-start | bytes 18436
  35.9 6.2 %copy-start.13 = (f32[1536]{0:T(1024)S(1)}, f32[1536]{0:T(1024)}, u32[]{:S(2)}) copy-start(f32[1536]{0:T(1024)} %get-tuple-element.16) | copy-start | bytes 18436
  35.9 6.2 %copy-start.14 = (f32[1536]{0:T(1024)S(1)}, f32[1536]{0:T(1024)}, u32[]{:S(2)}) copy-start(f32[1536]{0:T(1024)} %get-tuple-element.17) | copy-start | bytes 18436
  35.9 6.2 %copy-start.15 = (f32[1536]{0:T(1024)S(1)}, f32[1536]{0:T(1024)}, u32[]{:S(2)}) copy-start(f32[1536]{0:T(1024)} %get-tuple-element.18) | copy-start | bytes 18436
  35.9 6.2 %copy-start.16 = (f32[1536]{0:T(1024)S(1)}, f32[1536]{0:T(1024)}, u32[]{:S(2)}) copy-start(f32[1536]{0:T(1024)} %get-tuple-element.19) | copy-start | bytes 18436
  35.9 6.2 %copy-start.17 = (f32[1536]{0:T(1024)S(1)}, f32[1536]{0:T(1024)}, u32[]{:S(2)}) copy-start(f32[1536]{0:T(1024)} %get-tuple-element.20) | copy-start | bytes 18436
  35.9 6.2 %copy-start.18 = (f32[1536]{0:T(1024)S(1)}, f32[1536]{0:T(1024)}, u32[]{:S(2)}) copy-start(f32[1536]{0:T(1024)} %get-tuple-element.21) | copy-start | bytes 18436
  35.9 6.2 %copy-start.19 = (f32[1536]{0:T(1024)S(1)}, f32[1536]{0:T(1024)}, u32[]{:S(2)}) copy-start(f32[1536]{0:T(1024)} %get-tuple-element.22) | copy-start | bytes 18436
  35.9 6.2 %copy-start.20 = (f32[1536]{0:T(1024)S(1)}, f32[1536]{0:T(1024)}, u32[]{:S(2)}) copy-start(f32[1536]{0:T(1024)} %get-tuple-element.23) | copy-start | bytes 18436
  87.0 1.9 copy-start.4
  88.9 5.6 %copy-start.6 = (f32[16,32,32]{2,1,0:T(8,128)S(1)}, f32[16,32,32]{2,1,0:T(8,128)}, u32[]{:S(2)}) copy-start(f32[16,32,32]{2,1,0:T(8,128)} %fusion.16) | copy-start | bytes 196612
  188.1 5.8 %copy-start.21 = (bf16[16,64,512]{2,1,0:T(8,128)(2,1)S(1)}, bf16[16,64,512]{2,1,0:T(8,128)(2,1)}, u32[]{:S(2)}) copy-start(bf16[16,64,512]{2,1,0:T(8,128)(2,1)} %param.7) | copy-start | bytes 3145732
  188.1 5.8 %copy-start.22 = (bf16[1024,512]{1,0:T(8,128)(2,1)S(1)}, bf16[1024,512]{1,0:T(8,128)(2,1)}, u32[]{:S(2)}) copy-start(bf16[1024,512]{1,0:T(8,128)(2,1)} %param.11) | copy-start | bytes 3145732
  188.1 5.8 %copy-start.23 = (f32[512]{0:T(512)S(1)}, f32[512]{0:T(512)}, u32[]{:S(2)}) copy-start(f32[512]{0:T(512)} %param.13) | copy-start | bytes 6148
  188.1 5.8 %copy-start.24 = (f32[512]{0:T(512)S(1)}, f32[512]{0:T(512)}, u32[]{:S(2)}) copy-start(f32[512]{0:T(512)} %param.12) | copy-start | bytes 6148
Sparse Core Ops, SparseCore 0:
  95.5 92.5 all-reduce.1
where the time goes:
time: 204 us; the launch traced here: 203 us
  blocking collectives  60.9 us (30%)
  other arithmetic  36.1 us (18%)
  waiting for transfers between devices  31.1 us (15%)
  local copies, waits for them, and re-layouts  29.4 us (14%)
  matrix products  22.8 us (11%)
  between operations  13.8 us (7%)
  starting transfers between devices  9.01 us (4%)
    psum x1, blocking collectives, body(): lax.psum((jnp.concatenate([plain_state, scaled_state], 0), jnp.concatenat...  60.9 us
    psum x1, waiting for transfers between devices, body(): lax.psum((jnp.concatenate([plain_state, scaled_state], 0), jnp.concatenat...  27.5 us
    convert_element_type x1, other arithmetic, aggregate(): summed.astype(jnp.bfloat16)  24 us
    reshape x1, local copies, waits for them, and re-layouts, aggregate(): summed.astype(jnp.bfloat16)  9.4 us
    convert_element_type x1, local copies, waits for them, and re-layouts, aggregate(): summed.astype(jnp.bfloat16)  8.57 us
    ppermute x2, starting transfers between devices, padded_2(): before = lax.ppermute(last, axis, up)  6.24 us
    dot_general x1, matrix products, body(): jnp.einsum('nhd,hde->nhe', queries, states, precision=lax.Precision.HIGHEST)  5.75 us
    add x1, other arithmetic, feature_map(): return jax.nn.elu(inputs.astype(jnp.float32)) + 1.0  5.57 us
  transfers between devices with their start and end apart: 5, of which 3 were waited for; matrix products, arithmetic and copies ran while one was open for 8% of the time, Pallas kernels for 0%

commit v1 on v0

v1 whole, which is shorter than its diff:
```python
import functools

import jax
import jax.numpy as jnp
from jax import lax
from jax.experimental import pallas as pl
from jax.experimental.pallas import tpu as pltpu
from jax.sharding import PartitionSpec as P

HEAD_DIM = 32
PACK = 8 * HEAD_DIM
LANES = 128
SUB = 16
BF = jnp.bfloat16
F32 = jnp.float32
WAYS = ((1, 0), (-1, 0), (0, 1), (0, -1), (1, 1), (1, -1), (-1, 1), (-1, -1))


def iota(shape, dim):
    return lax.broadcasted_iota(jnp.int32, shape, dim)


def dot(a, b):
    return jnp.dot(a, b, preferred_element_type=F32)


def feature_map(u):
    return jnp.where(u > 0, u + 1.0, jnp.exp(jnp.minimum(u, 0.0)))


def one_hot(mask):
    return jnp.where(mask, 1.0, 0.0).astype(BF)


def kernel(
    n_rows, n_cols,
    tok_ref, w_ref, dk_ref, gk_ref, pw_ref, gain_ref, bias_ref,
    out_ref,
    stage_e, stage_c, halo_e, halo_c, halo_r, wq, taps, gbd, res, trip, spread, kfeat, acc,
    part, rs, ar_src, ar, ag,
    halo_send, halo_recv, red_send, red_recv,
):
    height, breadth, d = tok_ref.shape
    inner = breadth // SUB
    wide = inner + 4
    amount = height * breadth
    n_pack = d // PACK
    mr, mc = lax.axis_index("rows"), lax.axis_index("cols")

    def exists(way):
        r, c = mr + way[0], mc + way[1]
        return (r >= 0) & (r < n_rows) & (c >= 0) & (c < n_cols)

    def at(r, c):
        return {"rows": r, "cols": c}

    MESH = pl.DeviceIdType.MESH
    barrier = pltpu.get_barrier_semaphore()
    for k in range(1, n_rows):
        pl.semaphore_signal(barrier, inc=1, device_id=at(lax.rem(mr + k, n_rows), mc), device_id_type=MESH)
    for k in range(1, n_cols):
        pl.semaphore_signal(barrier, inc=1, device_id=at(mr, lax.rem(mc + k, n_cols)), device_id_type=MESH)
    for way in WAYS[4:]:
        @pl.when(exists(way))
        def _():
            pl.semaphore_signal(barrier, inc=1, device_id=at(mr + way[0], mc + way[1]), device_id_type=MESH)

    rows_out = 2 * 2 * height + 4 * SUB
    m = iota((rows_out, amount), 0)
    src = iota((rows_out, amount), 1)
    e = 2 * height
    right = (m >= e).astype(jnp.int32)
    me_ = m - right * e
    edge = (me_ // 2) * breadth + (me_ % 2) + right * (breadth - 2)
    cm = m - 2 * e
    ci, cr = cm // SUB, cm % SUB
    corner = ((cr // 2) + (ci // 2) * (height - 2)) * breadth + (cr % 2) + (ci % 2) * (breadth - 2)
    want = jnp.where(m < 2 * e, edge, jnp.where(cr < 4, corner, -1))
    sel = dot(one_hot(want == src), tok_ref[...].reshape(amount, d)).astype(BF)
    stage_e[...] = sel[: 2 * e].reshape(2, e, d)
    stage_c[...] = sel[2 * e :].reshape(4, SUB, d)

    moves = (
        (tok_ref.at[pl.ds(height - 2, 2)], halo_r.at[0]),
        (tok_ref.at[pl.ds(0, 2)], halo_r.at[1]),
        (stage_e.at[1], halo_e.at[0]),
        (stage_e.at[0], halo_e.at[1]),
        (stage_c.at[3], halo_c.at[0]),
        (stage_c.at[2], halo_c.at[1]),
        (stage_c.at[1], halo_c.at[2]),
        (stage_c.at[0], halo_c.at[3]),
    )

    def halo_copy(i):
        way = WAYS[i]
        return pltpu.make_async_remote_copy(
            src_ref=moves[i][0], dst_ref=moves[i][1],
            send_sem=halo_send.at[i], recv_sem=halo_recv.at[i],
            device_id=at(mr + way[0], mc + way[1]), device_id_type=MESH,
        )

    n_diag = sum(exists(way).astype(jnp.int32) for way in WAYS[4:])
    pl.semaphore_wait(barrier, n_rows - 1 + n_cols - 1 + n_diag)
    for i, way in enumerate(WAYS):
        @pl.when(exists(way))
        def _():
            halo_copy(i).start()

        @pl.when(jnp.logical_not(exists((-way[0], -way[1]))))
        def _():
            dst = moves[i][1]
            dst[...] = jnp.zeros(dst.shape, BF)

    third = 3 * PACK
    row, col = iota((third, third), 0), iota((third, third), 1)
    rem = col % PACK
    perm = one_hot(row == (rem // HEAD_DIM) * (3 * HEAD_DIM) + (col // PACK) * HEAD_DIM + rem % HEAD_DIM)
    for i in range(n_pack):
        wp = dot(w_ref[:, third * i : third * (i + 1)], perm).astype(BF)
        tp = dot(dk_ref[:, third * i : third * (i + 1)].astype(BF), perm)
        for t in range(3):
            lo = t * d + i * PACK
            wq[:, lo : lo + PACK] = wp[:, t * PACK : (t + 1) * PACK]
            for tap in range(25):
                taps[tap, :, lo : lo + PACK] = jnp.broadcast_to(
                    tp[tap : tap + 1, t * PACK : (t + 1) * PACK], (SUB, PACK)
                ).astype(BF)
    prow, pcol = iota((PACK, PACK), 0), iota((PACK, PACK), 1)
    same = prow // HEAD_DIM == pcol // HEAD_DIM
    tiled_eye = one_hot(iota((HEAD_DIM, PACK), 1) % HEAD_DIM == iota((HEAD_DIM, PACK), 0))
    for t in range(3):
        for i in range(n_pack):
            g = jnp.concatenate([gk_ref[3 * (8 * i + h) + t] for h in range(8)], axis=0)
            gbd[t * n_pack + i] = jnp.where(same, dot(g, tiled_eye), 0.0).astype(BF)

    for i, way in enumerate(WAYS):
        @pl.when(exists((-way[0], -way[1])))
        def _():
            halo_copy(i).wait_recv()

    halo = jnp.concatenate([halo_e[...].reshape(2 * e, d), halo_c[...].reshape(4 * SUB, d)], axis=0)
    base = 2 * breadth
    size_m, size_k = 2 * wide * SUB, base + 2 * e + 4 * SUB
    m, src = iota((size_m, size_k), 0), iota((size_m, size_k), 1)
    which = m // (wide * SUB)
    jj, s = (m // SUB) % wide, m % SUB
    c = inner * s + jj - 2
    for p in range(height // 2 + 2):
        if p == 0:
            pair, lo, hi, line = halo_r[0], base + 2 * e, base + 2 * e + SUB, 0
        elif p == height // 2 + 1:
            pair, lo, hi, line = halo_r[1], base + 2 * e + 2 * SUB, base + 2 * e + 3 * SUB, 0
        else:
            pair, lo, hi, line = tok_ref[2 * p - 2 : 2 * p], base, base + e, 2 * p - 2
        side = 2 * (which + line)
        want = jnp.where(c < 0, lo + side + c + 2, jnp.where(c >= breadth, hi + side + c - breadth, which * breadth + c))
        x = jnp.concatenate([pair.reshape(base, d), halo], axis=0)
        y = dot(one_hot(want == src), x).astype(BF)
        if 0 < p < height // 2 + 1:
            res[2 * p - 2 : 2 * p] = y.reshape(2, wide, SUB, d)[:, 2 : 2 + inner]
        trip[2 * p : 2 * p + 2] = dot(y, wq[...]).astype(BF).reshape(2, wide, SUB, 3 * d)

    zrow, zcol = iota((PACK, LANES), 0), iota((PACK, LANES), 1)
    ones = jnp.ones((amount, LANES), BF)
    dn = (((0,), (0,)), ((), ()))

    def local_states(z, get_k, get_v):
        total = jnp.zeros((HEAD_DIM, LANES), F32)
        pieces = []
        for i in range(n_pack):
            k, v = get_k(i), get_v(i)
            st = lax.dot_general(k, v, dn, preferred_element_type=F32)
            pieces.append(jnp.sum(jnp.where(same, st, 0.0).reshape(8, HEAD_DIM, PACK), axis=0))
            tot = lax.dot_general(k, ones, dn, preferred_element_type=F32)
            tot = jnp.where(zcol == 8 * i + zrow // HEAD_DIM, tot, 0.0)
            total = total + jnp.sum(tot.reshape(8, HEAD_DIM, LANES), axis=0)
        flat = jnp.concatenate(pieces + [total], axis=1)
        step = HEAD_DIM // n_cols
        for q in range(n_cols):
            part[z, q] = flat[q * step : (q + 1) * step]

    def rs_copy(z, k):
        peer = lax.rem(mc + k, n_cols)
        return pltpu.make_async_remote_copy(
            src_ref=part.at[z, peer], dst_ref=rs.at[z, k - 1],
            send_sem=red_send.at[z, 0, k - 1], recv_sem=red_recv.at[z, 0, k - 1],
            device_id=at(mr, peer), device_id_type=MESH,
        )

    def ar_copy(z, k):
        return pltpu.make_async_remote_copy(
            src_ref=ar_src.at[z], dst_ref=ar.at[z, k - 1],
            send_sem=red_send.at[z, 1, k - 1], recv_sem=red_recv.at[z, 1, k - 1],
            device_id=at(lax.rem(mr + k, n_rows), mc), device_id_type=MESH,
        )

    def ag_copy(z, k):
        return pltpu.make_async_remote_copy(
            src_ref=ag.at[z, mc], dst_ref=ag.at[z, mc],
            send_sem=red_send.at[z, 2, k - 1], recv_sem=red_recv.at[z, 2, k - 1],
            device_id=at(mr, lax.rem(mc + k, n_cols)), device_id_type=MESH,
        )

    def ag_wait(z, k):
        sender = lax.rem(mc - k + n_cols, n_cols)
        pltpu.make_async_remote_copy(
            src_ref=ag.at[z, mc], dst_ref=ag.at[z, sender],
            send_sem=red_send.at[z, 2, k - 1], recv_sem=red_recv.at[z, 2, k - 1],
            device_id=at(mr, sender), device_id_type=MESH,
        ).wait_recv()

    def reduce_1(z):
        for k in range(1, n_cols):
            rs_copy(z, k).start()

    def reduce_2(z):
        total = part[z, mc]
        for k in range(1, n_cols):
            rs_copy(z, k).wait_recv()
            total = total + rs[z, k - 1]
        ar_src[z] = total
        for k in range(1, n_rows):
            ar_copy(z, k).start()

    def reduce_3(z):
        total = ar_src[z]
        for k in range(1, n_rows):
            ar_copy(z, k).wait_recv()
            total = total + ar[z, k - 1]
        ag[z, mc] = total
        for k in range(1, n_cols):
            ag_copy(z, k).start()

    def reduce_4(z):
        for k in range(1, n_cols):
            ag_wait(z, k)
        return jnp.concatenate([ag[z, q] for q in range(n_cols)], axis=0)

    def conv(first, last):
        def chunk(ch, _):
            lanes = pl.ds(pl.multiple_of(ch * LANES, LANES), LANES)
            w = [taps[t, :, lanes] for t in range(25)]

            def line(r, _):
                sums = [None] * inner
                for a in range(5):
                    xs = [trip[r + a, jj, :, lanes] for jj in range(wide)]
                    for j in range(inner):
                        term = xs[j] * w[5 * a]
                        for b in range(1, 5):
                            term = term + xs[j + b] * w[5 * a + b]
                        sums[j] = term if a == 0 else sums[j] + term
                for j in range(inner):
                    spread[r, j, :, lanes] = sums[j]
                return 0

            lax.fori_loop(0, height, line, 0)
            return 0

        lax.fori_loop(first, last, chunk, 0)

    def native(t, i):
        lo = t * d + i * PACK
        return trip[2 : 2 + height, 2 : 2 + inner, :, lo : lo + PACK].reshape(amount, PACK)

    def grouped(t, i):
        lo = t * d + i * PACK
        return dot(spread[:, :, :, lo : lo + PACK].reshape(amount, PACK), gbd[t * n_pack + i]).astype(BF)

    def attend(z, flat, get_q):
        for i in range(n_pack):
            st = flat[:, i * PACK : (i + 1) * PACK]
            st = jnp.where(same, jnp.concatenate([st] * 8, axis=0), 0.0).astype(BF)
            head = one_hot(iota((LANES, PACK), 0) == 8 * i + iota((LANES, PACK), 1) // HEAD_DIM)
            tot = dot(flat[:, n_pack * PACK :].astype(BF), head)
            tot = jnp.where(same, jnp.concatenate([tot] * 8, axis=0), 0.0).astype(BF)
            q = feature_map(get_q(i).astype(F32)).astype(BF)
            att = (dot(q, st) / dot(q, tot)).astype(BF)
            add = dot(att, pw_ref[z * d + i * PACK : z * d + (i + 1) * PACK, :])
            if z == 0 and i == 0:
                acc[...] = add
            else:
                acc[...] += add

    n_chunk = d // LANES
    local_states(0, lambda i: feature_map(native(1, i).astype(F32)).astype(BF), lambda i: native(2, i))
    reduce_1(0)
    conv(n_chunk, 2 * n_chunk)
    reduce_2(0)
    conv(2 * n_chunk, 3 * n_chunk)
    reduce_3(0)
    local_states(1, lambda i: feature_map(grouped(1, i).astype(F32)).astype(BF), lambda i: grouped(2, i))
    reduce_1(1)
    conv(0, n_chunk)
    reduce_2(1)
    attend(0, reduce_4(0), lambda i: native(0, i))
    reduce_3(1)
    attend(1, reduce_4(1), lambda i: grouped(0, i))

    lines = 4
    size = lines * breadth
    m, src = iota((size, size), 0), iota((size, size), 1)
    cc = m % breadth
    back = one_hot(src == (m // breadth) * breadth + (cc % inner) * SUB + cc // inner)
    for b in range(height // lines):
        got = acc[b * size : (b + 1) * size, :] * gain_ref[...] + bias_ref[...]
        got = (got + res[b * lines : (b + 1) * lines].reshape(size, d).astype(F32)).astype(BF)
        out_ref[b * lines : (b + 1) * lines] = dot(back, got).astype(BF).reshape(lines, breadth, d)

    for i, way in enumerate(WAYS):
        @pl.when(exists(way))
        def _():
            halo_copy(i).wait_send()
    for z in range(2):
        for k in range(1, n_cols):
            rs_copy(z, k).wait_send()
            ag_copy(z, k).wait_send()
        for k in range(1, n_rows):
            ar_copy(z, k).wait_send()


def body(n_rows, n_cols, tokens, qkv_weight, depth_kernel, group_kernel, proj_weight, out_gain, out_bias):
    height, breadth, d = tokens.shape
    inner = breadth // SUB
    step = HEAD_DIM // n_cols
    msg = d + LANES
    most = max(n_rows, n_cols)
    vmem = pl.BlockSpec(memory_space=pltpu.VMEM)
    return pl.pallas_call(
        functools.partial(kernel, n_rows, n_cols),
        out_shape=jax.ShapeDtypeStruct((height, breadth, d), BF),
        in_specs=[vmem] * 7,
        out_specs=vmem,
        scratch_shapes=[
            pltpu.VMEM((2, 2 * height, d), BF),
            pltpu.VMEM((4, SUB, d), BF),
            pltpu.VMEM((2, 2 * height, d), BF),
            pltpu.VMEM((4, SUB, d), BF),
            pltpu.VMEM((2, 2, breadth, d), BF),
            pltpu.VMEM((d, 3 * d), BF),
            pltpu.VMEM((25, SUB, 3 * d), BF),
            pltpu.VMEM((3 * d // PACK, PACK, PACK), BF),
            pltpu.VMEM((height, inner, SUB, d), BF),
            pltpu.VMEM((height + 4, inner + 4, SUB, 3 * d), BF),
            pltpu.VMEM((height, inner, SUB, 3 * d), BF),
            pltpu.VMEM((8, LANES), BF),
            pltpu.VMEM((height * breadth, d), F32),
            pltpu.VMEM((2, n_cols, step, msg), F32),
            pltpu.VMEM((2, n_cols - 1, step, msg), F32),
            pltpu.VMEM((2, step, msg), F32),
            pltpu.VMEM((2, n_rows - 1, step, msg), F32),
            pltpu.VMEM((2, n_cols, step, msg), F32),
            pltpu.SemaphoreType.DMA((8,)),
            pltpu.SemaphoreType.DMA((8,)),
            pltpu.SemaphoreType.DMA((2, 3, most)),
            pltpu.SemaphoreType.DMA((2, 3, most)),
        ],
        compiler_params=pltpu.CompilerParams(
            collective_id=0, has_side_effects=True, vmem_limit_bytes=56 * 1024 * 1024
        ),
        name="attention_module",
    )(tokens, qkv_weight, depth_kernel, group_kernel, proj_weight, out_gain[None, :], out_bias[None, :])


def solution(mesh):
    placed = (P(("groups", "rows"), "cols", None), P(), P(), P(), P(), P(), P())
    return jax.shard_map(
        functools.partial(body, mesh.shape["rows"], mesh.shape["cols"]),
        mesh=mesh,
        in_specs=placed,
        out_specs=P(("groups", "rows"), "cols", None),
        check_vma=False,
    )
```

time: 204 us -> 51.2 us (0.25)
  blocking collectives: 60.9 us -> 0 us
  Pallas kernels: 0 us -> 46.5 us
  other arithmetic: 36.1 us -> 0 us
  waiting for transfers between devices: 31.1 us -> 0 us
  local copies, waits for them, and re-layouts: 29.4 us -> 4.55 us
  matrix products: 22.8 us -> 0 us
  between operations: 13.8 us -> 0.01 us
  starting transfers between devices: 9.01 us -> 0 us
    psum x1 -> x0, blocking collectives: 60.9 us -> none  [body(): lax.psum((jnp.concatenate([plain_state, scaled_state], 0), jnp.concatenat...]
    pallas_call x0 -> x1, Pallas kernels: none -> 46.5 us  [body(): pl.pallas_call(functools.partial(kernel, n_rows, n_cols), out_shape=jax.S...]
    psum x1 -> x0, waiting for transfers between devices: 27.5 us -> none  [body(): lax.psum((jnp.concatenate([plain_state, scaled_state], 0), jnp.concatenat...]
    convert_element_type x1 -> x0, other arithmetic: 24 us -> none  [aggregate(): summed.astype(jnp.bfloat16)]
    dot_general x7 -> x0, matrix products: 22.8 us -> none  [the longest x1 5.75 us: body(): jnp.einsum('nhd,hde->nhe', queries, states, precision=lax.Precision.HIGHEST)]
    convert_element_type x2 -> x0, local copies, waits for them, and re-layouts: 13.3 us -> none  [the longest x1 8.57 us: aggregate(): summed.astype(jnp.bfloat16)]
    reshape x1 -> x0, local copies, waits for them, and re-layouts: 9.4 us -> none  [aggregate(): summed.astype(jnp.bfloat16)]
    ppermute x4 -> x0, starting transfers between devices: 9.01 us -> none  [the longest x2 6.24 us: padded_2(): before = lax.ppermute(last, axis, up)]
  transfers between devices with their start and end apart: 5 -> 0, of which waited for: 3 -> 0; matrix products, arithmetic and copies ran while one was open for 8% -> 0% of each run, Pallas kernels for 0% -> 0%
where the time goes in v1:
time: 51.2 us; the launch traced here: 51 us
  Pallas kernels  46.5 us (91%)
  local copies, waits for them, and re-layouts  4.55 us (9%)
    pallas_call x1, Pallas kernels, body(): pl.pallas_call(functools.partial(kernel, n_rows, n_cols), out_shape=jax.S...  46.5 us
    unnamed x2, local copies, waits for them, and re-layouts  4.55 us

profile of v1, /device:TPU:0, one launch (start us, length us, event | category | flops | bytes accessed | tf_op | source)
XLA Modules:
  0.0 51.0 jit_solution(5227991676157694624)
XLA Ops:
  0.0 2.3 %copy.8.gk_ref = bf16[48,32,32]{2,1,0:T(8,128)(2,1)} copy(bf16[48,32,32]{0,2,1:T(8,128)(2,1)} %param.10) | data formatting | bytes 196608 | tf_op args[3]
  2.3 46.5 %attention_module.1 = bf16[16,64,512]{2,1,0:T(8,128)(2,1)} custom-call(bf16[16,64,512]{2,1,0:T(8,128)(2,1)} %tok_ref.1, bf16[512,1536]{1,0:T(8,128)(2,1)} %w_ref.1, f32[25,1536]{1,0:T(8,128)} %dk_ref.1, bf16[48,32,32]{2,1,0:T(8,128)(2,1)} %copy.8.gk_ref, bf16[1024,512]{1,0:T(8,128)(2,1)} %pw_ref.1, f32[1,512]{1,0:T(1,128)} %bitcast.2, f32[1,512]{1,0:T(1,128)} %bitcast.3), custom_call_target="tpu_custom_call" | custom-call | tf_op jit(solution)/shard_map/attention_module/pallas_call | solution.py:329
  48.7 2.3 %copy.10 = bf16[16,64,512]{2,1,0:T(8,128)(2,1)} copy(bf16[16,64,512]{2,1,0:T(8,128)(2,1)} %attention_module.1) | data formatting | bytes 2097152

commit v2 on v1

--- a/solution.py
+++ b/solution.py
@@ -36,7 +36,7 @@
     n_rows, n_cols,
     tok_ref, w_ref, dk_ref, gk_ref, pw_ref, gain_ref, bias_ref,
     out_ref,
-    stage_e, stage_c, halo_e, halo_c, halo_r, wq, taps, gbd, res, trip, spread, kfeat, acc,
+    stage_e, stage_c, halo_e, halo_c, halo_r, wq, taps, gbd, res, trip, spread, acc,
     part, rs, ar_src, ar, ag,
     halo_send, halo_recv, red_send, red_recv,
 ):
@@ -99,66 +99,40 @@
             device_id=at(mr + way[0], mc + way[1]), device_id_type=MESH,
         )
 
-    n_diag = sum(exists(way).astype(jnp.int32) for way in WAYS[4:])
-    pl.semaphore_wait(barrier, n_rows - 1 + n_cols - 1 + n_diag)
-    for i, way in enumerate(WAYS):
-        @pl.when(exists(way))
-        def _():
-            halo_copy(i).start()
-
-        @pl.when(jnp.logical_not(exists((-way[0], -way[1]))))
-        def _():
-            dst = moves[i][1]
-            dst[...] = jnp.zeros(dst.shape, BF)
-
     third = 3 * PACK
     row, col = iota((third, third), 0), iota((third, third), 1)
     rem = col % PACK
     perm = one_hot(row == (rem // HEAD_DIM) * (3 * HEAD_DIM) + (col // PACK) * HEAD_DIM + rem % HEAD_DIM)
     for i in range(n_pack):
         wp = dot(w_ref[:, third * i : third * (i + 1)], perm).astype(BF)
-        tp = dot(dk_ref[:, third * i : third * (i + 1)].astype(BF), perm)
         for t in range(3):
             lo = t * d + i * PACK
             wq[:, lo : lo + PACK] = wp[:, t * PACK : (t + 1) * PACK]
-            for tap in range(25):
-                taps[tap, :, lo : lo + PACK] = jnp.broadcast_to(
-                    tp[tap : tap + 1, t * PACK : (t + 1) * PACK], (SUB, PACK)
-                ).astype(BF)
     prow, pcol = iota((PACK, PACK), 0), iota((PACK, PACK), 1)
     same = prow // HEAD_DIM == pcol // HEAD_DIM
-    tiled_eye = one_hot(iota((HEAD_DIM, PACK), 1) % HEAD_DIM == iota((HEAD_DIM, PACK), 0))
-    for t in range(3):
-        for i in range(n_pack):
-            g = jnp.concatenate([gk_ref[3 * (8 * i + h) + t] for h in range(8)], axis=0)
-            gbd[t * n_pack + i] = jnp.where(same, dot(g, tiled_eye), 0.0).astype(BF)
-
+    base = 2 * breadth
+    size_m = 2 * wide * SUB
+    m, src = iota((size_m, base), 0), iota((size_m, base), 1)
+    which = m // (wide * SUB)
+    c = inner * (m % SUB) + (m // SUB) % wide - 2
+    inside = (c >= 0) & (c < breadth)
+    place = one_hot((which * breadth + c == src) & inside)
+    for p in range(height // 2):
+        y = dot(place, tok_ref[2 * p : 2 * p + 2].reshape(base, d)).astype(BF)
+        res[2 * p : 2 * p + 2] = y.reshape(2, wide, SUB, d)[:, 2 : 2 + inner]
+        trip[2 * p + 2 : 2 * p + 4] = dot(y, wq[...]).astype(BF).reshape(2, wide, SUB, 3 * d)
+
+    n_diag = sum(exists(way).astype(jnp.int32) for way in WAYS[4:])
+    pl.semaphore_wait(barrier, n_rows - 1 + n_cols - 1 + n_diag)
     for i, way in enumerate(WAYS):
-        @pl.when(exists((-way[0], -way[1])))
-        def _():
-            halo_copy(i).wait_recv()
-
-    halo = jnp.concatenate([halo_e[...].reshape(2 * e, d), halo_c[...].reshape(4 * SUB, d)], axis=0)
-    base = 2 * breadth
-    size_m, size_k = 2 * wide * SUB, base + 2 * e + 4 * SUB
-    m, src = iota((size_m, size_k), 0), iota((size_m, size_k), 1)
-    which = m // (wide * SUB)
-    jj, s = (m // SUB) % wide, m % SUB
-    c = inner * s + jj - 2
-    for p in range(height // 2 + 2):
-        if p == 0:
-            pair, lo, hi, line = halo_r[0], base + 2 * e, base + 2 * e + SUB, 0
-        elif p == height // 2 + 1:
-            pair, lo, hi, line = halo_r[1], base + 2 * e + 2 * SUB, base + 2 * e + 3 * SUB, 0
-        else:
-            pair, lo, hi, line = tok_ref[2 * p - 2 : 2 * p], base, base + e, 2 * p - 2
-        side = 2 * (which + line)
-        want = jnp.where(c < 0, lo + side + c + 2, jnp.where(c >= breadth, hi + side + c - breadth, which * breadth + c))
-        x = jnp.concatenate([pair.reshape(base, d), halo], axis=0)
-        y = dot(one_hot(want == src), x).astype(BF)
-        if 0 < p < height // 2 + 1:
-            res[2 * p - 2 : 2 * p] = y.reshape(2, wide, SUB, d)[:, 2 : 2 + inner]
-        trip[2 * p : 2 * p + 2] = dot(y, wq[...]).astype(BF).reshape(2, wide, SUB, 3 * d)
+        @pl.when(exists(way))
+        def _():
+            halo_copy(i).start()
+
+        @pl.when(jnp.logical_not(exists((-way[0], -way[1]))))
+        def _():
+            dst = moves[i][1]
+            dst[...] = jnp.zeros(dst.shape, BF)
 
     zrow, zcol = iota((PACK, LANES), 0), iota((PACK, LANES), 1)
     ones = jnp.ones((amount, LANES), BF)
@@ -282,9 +256,55 @@
             else:
                 acc[...] += add
 
-    n_chunk = d // LANES
     local_states(0, lambda i: feature_map(native(1, i).astype(F32)).astype(BF), lambda i: native(2, i))
     reduce_1(0)
+    for i in range(n_pack):
+        tp = dot(dk_ref[:, third * i : third * (i + 1)].astype(BF), perm)
+        for t in range(3):
+            lo = t * d + i * PACK
+            for tap in range(25):
+                taps[tap, :, lo : lo + PACK] = jnp.broadcast_to(
+                    tp[tap : tap + 1, t * PACK : (t + 1) * PACK], (SUB, PACK)
+                ).astype(BF)
+    n_group = gk_ref.shape[2]
+    gk = gk_ref[...].reshape(HEAD_DIM * HEAD_DIM, n_group)
+    grow, gcol = iota((n_group, PACK), 0), iota((n_group, PACK), 1)
+    keep = iota((HEAD_DIM * HEAD_DIM, PACK), 0) % HEAD_DIM == iota((HEAD_DIM * HEAD_DIM, PACK), 1) % HEAD_DIM
+    for t in range(3):
+        for i in range(n_pack):
+            g = dot(gk, one_hot(grow == 3 * (8 * i + gcol // HEAD_DIM) + t))
+            g = jnp.sum(jnp.where(keep, g, 0.0).reshape(HEAD_DIM, HEAD_DIM, PACK), axis=1)
+            gbd[t * n_pack + i] = jnp.where(same, jnp.concatenate([g] * 8, axis=0), 0.0).astype(BF)
+
+    for i, way in enumerate(WAYS):
+        @pl.when(exists((-way[0], -way[1])))
+        def _():
+            halo_copy(i).wait_recv()
+
+
+    corners = halo_c[...].reshape(4 * SUB, d)
+    size_k = base + 4 * SUB
+    m, src = iota((size_m, size_k), 0), iota((size_m, size_k), 1)
+    which = m // (wide * SUB)
+    c = inner * (m % SUB) + (m // SUB) % wide - 2
+    for p in range(2):
+        lo = base + 2 * p * SUB + 2 * which
+        want = jnp.where(c < 0, lo + c + 2, jnp.where(c >= breadth, lo + SUB + c - breadth, which * breadth + c))
+        y = dot(one_hot(want == src), jnp.concatenate([halo_r[p].reshape(base, d), corners], axis=0)).astype(BF)
+        first = p * (height + 2)
+        trip[first : first + 2] = dot(y, wq[...]).astype(BF).reshape(2, wide, SUB, 3 * d)
+    sides = dot(halo_e[...].reshape(2 * e, d), wq[...])
+    spot = iota((SUB, 3 * d), 0)
+    masks = (one_hot(spot == 0), one_hot(spot == SUB - 1))
+    for r in range(height):
+        for side in range(2):
+            for b in range(2):
+                at_row = side * e + 2 * r + b
+                jj = side * (inner + 2) + b
+                line = jnp.broadcast_to(sides[at_row : at_row + 1], (SUB, 3 * d)).astype(BF)
+                trip[r + 2, jj] = trip[r + 2, jj] + line * masks[side]
+
+    n_chunk = d // LANES
     conv(n_chunk, 2 * n_chunk)
     reduce_2(0)
     conv(2 * n_chunk, 3 * n_chunk)
@@ -343,7 +363,6 @@
             pltpu.VMEM((height, inner, SUB, d), BF),
             pltpu.VMEM((height + 4, inner + 4, SUB, 3 * d), BF),
             pltpu.VMEM((height, inner, SUB, 3 * d), BF),
-            pltpu.VMEM((8, LANES), BF),
             pltpu.VMEM((height * breadth, d), F32),
             pltpu.VMEM((2, n_cols, step, msg), F32),
             pltpu.VMEM((2, n_cols - 1, step, msg), F32),
@@ -359,7 +378,7 @@
             collective_id=0, has_side_effects=True, vmem_limit_bytes=56 * 1024 * 1024
         ),
         name="attention_module",
-    )(tokens, qkv_weight, depth_kernel, group_kernel, proj_weight, out_gain[None, :], out_bias[None, :])
+    )(tokens, qkv_weight, depth_kernel, jnp.transpose(group_kernel, (1, 2, 0)), proj_weight, out_gain[None, :], out_bias[None, :])
 
 
 def solution(mesh):

time: 51.2 us -> 48.7 us (0.951)
  local copies, waits for them, and re-layouts: 4.55 us -> 2.29 us
    unnamed x2 -> x1, local copies, waits for them, and re-layouts: 4.55 us -> 2.29 us
where the time goes in v2:
time: 48.7 us; the launch traced here: 48.5 us
  Pallas kernels  46.2 us (95%)
  local copies, waits for them, and re-layouts  2.29 us (5%)
    pallas_call x1, Pallas kernels, body(): pl.pallas_call(functools.partial(kernel, n_rows, n_cols), out_shape=jax.S...  46.2 us
    unnamed x1, local copies, waits for them, and re-layouts  2.29 us

profile of v2, /device:TPU:0, one launch (start us, length us, event | category | flops | bytes accessed | tf_op | source)
XLA Modules:
  0.0 48.5 jit_solution(4382313898335952635)
XLA Ops:
  0.0 46.2 %attention_module.1 = bf16[16,64,512]{2,1,0:T(8,128)(2,1)} custom-call(bf16[16,64,512]{2,1,0:T(8,128)(2,1)} %tok_ref.1, bf16[512,1536]{1,0:T(8,128)(2,1)} %w_ref.1, f32[25,1536]{1,0:T(8,128)} %dk_ref.1, bf16[32,32,48]{2,1,0:T(8,128)(2,1)} %bitcast.3, bf16[1024,512]{1,0:T(8,128)(2,1)} %pw_ref.1, f32[1,512]{1,0:T(1,128)} %bitcast.4, f32[1,512]{1,0:T(1,128)} %bitcast.5), custom_call_target="tpu_custom_call" | custom-call | tf_op jit(solution)/shard_map/attention_module/pallas_call | solution.py:349
  46.2 2.3 %copy.9 = bf16[16,64,512]{2,1,0:T(8,128)(2,1)} copy(bf16[16,64,512]{2,1,0:T(8,128)(2,1)} %attention_module.1) | data formatting | bytes 2097152

commit v3 on v2

--- a/solution.py
+++ b/solution.py
@@ -228,7 +228,7 @@
                     spread[r, j, :, lanes] = sums[j]
                 return 0
 
-            lax.fori_loop(0, height, line, 0)
+            lax.fori_loop(0, height, line, 0, unroll=2)
             return 0
 
         lax.fori_loop(first, last, chunk, 0)
@@ -311,10 +311,11 @@
     reduce_3(0)
     local_states(1, lambda i: feature_map(grouped(1, i).astype(F32)).astype(BF), lambda i: grouped(2, i))
     reduce_1(1)
-    conv(0, n_chunk)
+    conv(0, n_chunk // 2)
     reduce_2(1)
+    conv(n_chunk // 2, n_chunk)
+    reduce_3(1)
     attend(0, reduce_4(0), lambda i: native(0, i))
-    reduce_3(1)
     attend(1, reduce_4(1), lambda i: grouped(0, i))
 
     lines = 4

time: 48.7 us -> 45.3 us (0.930)
  Pallas kernels: 46.2 us -> 42.9 us
    pallas_call x1, Pallas kernels: 46.2 us -> 42.9 us  [body(): pl.pallas_call(functools.partial(kernel, n_rows, n_cols), out_shape=jax.S...]
where the time goes in v3:
time: 45.3 us; the launch traced here: 45.2 us
  Pallas kernels  42.9 us (95%)
  local copies, waits for them, and re-layouts  2.29 us (5%)
    pallas_call x1, Pallas kernels, body(): pl.pallas_call(functools.partial(kernel, n_rows, n_cols), out_shape=jax.S...  42.9 us
    unnamed x1, local copies, waits for them, and re-layouts  2.29 us

profile of v3, /device:TPU:0, one launch (start us, length us, event | category | flops | bytes accessed | tf_op | source)
XLA Modules:
  0.0 45.2 jit_solution(7283253137701848932)
XLA Ops:
  0.0 42.9 %attention_module.1 = bf16[16,64,512]{2,1,0:T(8,128)(2,1)} custom-call(bf16[16,64,512]{2,1,0:T(8,128)(2,1)} %tok_ref.1, bf16[512,1536]{1,0:T(8,128)(2,1)} %w_ref.1, f32[25,1536]{1,0:T(8,128)} %dk_ref.1, bf16[32,32,48]{2,1,0:T(8,128)(2,1)} %bitcast.3, bf16[1024,512]{1,0:T(8,128)(2,1)} %pw_ref.1, f32[1,512]{1,0:T(1,128)} %bitcast.4, f32[1,512]{1,0:T(1,128)} %bitcast.5), custom_call_target="tpu_custom_call" | custom-call | tf_op jit(solution)/shard_map/attention_module/pallas_call | solution.py:350
  42.9 2.3 %copy.9 = bf16[16,64,512]{2,1,0:T(8,128)(2,1)} copy(bf16[16,64,512]{2,1,0:T(8,128)(2,1)} %attention_module.1) | data formatting | bytes 2097152
